TPU v7x, 512 devices: a whole 4x4x16 slice. The times are simulated.
512 devices in a mesh: bl: 32 (over y, x, core), dir: 16 (over z).
Axes of the slice: x: 4, y: 4, z: 16, core: 2. Of those that a mesh axis runs over, the one named last changes fastest.
Arguments:
- visibilities: float32 [8, 16, 8192], P(None, 'dir', 'bl'), may hold values from -24 to 24
- coherencies: bfloat16 [32, 8, 16, 8192], P('dir', None, None, 'bl'), may hold values from -6 to 6
- gain_offsets: float32 [32, 8, 512], P(None, None, 'bl'), may hold values from -1.5 to 1.5
- stations: int32 [2, 8192], P(None, 'bl'), may hold values from 0 to 511, as said below
- solve_order: int32 [32], replicated, may hold values from 0 to 31, each once
- counts: int32 [32], replicated, may hold values from 1 to 2
- damping: int32 [32], replicated, may hold values from 1 to 8
Outputs:
- gains: float32 [32, 8, 512], P(None, None, 'bl')
- residual: float32 [8, 16, 8192], P(None, 'dir', 'bl')
Inputs may be any that keep to these rules, and one draw needn't show every extreme that they name: Each baseline names two different stations. `solve_order`: each direction appears once.
All inputs are finite; a program needn't handle non-finite values.
Results may differ from a plain program's by a relative error of at most 0.0003.
Values may be sent and summed in bfloat16 or wider, within the bound.
A program may use at most 64 MiB of HBM per device.

v0:
```python
import jax
import jax.numpy as jnp
from jax import lax
from jax.sharding import PartitionSpec as P

LM_ITERS = 2
SOLVED = 4


def matrix_entry(mat, i, j):
    return (mat[4 * i + 2 * j], mat[4 * i + 2 * j + 1])


def matmul_two(left, right):
    pieces = []
    for i in (0, 1):
        for j in (0, 1):
            left_r0, left_i0 = matrix_entry(left, i, 0)
            left_r1, left_i1 = matrix_entry(left, i, 1)
            right_r0, right_i0 = matrix_entry(right, 0, j)
            right_r1, right_i1 = matrix_entry(right, 1, j)
            pieces.append(
                left_r0 * right_r0 - left_i0 * right_i0 + left_r1 * right_r1 - left_i1 * right_i1
            )
            pieces.append(
                left_r0 * right_i0 + left_i0 * right_r0 + left_r1 * right_i1 + left_i1 * right_r1
            )
    return jnp.stack(pieces)


def adjoint(mat):
    return jnp.stack([mat[0], -mat[1], mat[4], -mat[5], mat[2], -mat[3], mat[6], -mat[7]])


def apply_gains(gain_p, coher_now, gain_q):
    return matmul_two(matmul_two(gain_p, coher_now), adjoint(gain_q))


def gram_parts(gram):
    return jnp.stack([gram[0], gram[6], gram[2], gram[3]])


def station_terms(gain_p, gain_q, coher_now, target):
    z_rows = matmul_two(coher_now, adjoint(gain_q))
    y_rows = matmul_two(adjoint(coher_now), adjoint(gain_p))
    leading_endpoint = jnp.concatenate(
        [matmul_two(target, adjoint(z_rows)), gram_parts(matmul_two(z_rows, adjoint(z_rows)))], 0
    )
    second = jnp.concatenate(
        [
            matmul_two(adjoint(target), adjoint(y_rows)),
            gram_parts(matmul_two(y_rows, adjoint(y_rows))),
        ],
        0,
    )
    return (jnp.sum(leading_endpoint, axis=1), jnp.sum(second, axis=1))


def solve_station(gathered_sums, gain_now, damp_value):
    numerator = gathered_sums[:8] + damp_value * gain_now
    diag_a = gathered_sums[8] + damp_value
    diag_d = gathered_sums[9] + damp_value
    cross_r = gathered_sums[10]
    cross_i = gathered_sums[11]
    determinant = diag_a * diag_d - cross_r * cross_r - cross_i * cross_i
    zeros_row = jnp.zeros_like(determinant)
    inverse = (
        jnp.stack([diag_d, zeros_row, -cross_r, -cross_i, -cross_r, cross_i, diag_a, zeros_row])
        / determinant
    )
    return matmul_two(numerator, inverse)


def on_device(visibilities, coherencies, gain_offsets, stations, solve_order, counts, damping):
    identity = jnp.zeros((8,), jnp.float32).at[0].set(1.0).at[6].set(1.0)
    start = lax.all_gather(gain_offsets, "bl", axis=2, tiled=True) + identity[None, :, None]
    groups = lax.axis_size("bl")
    total_channels = coherencies.shape[2]
    station_count = start.shape[2]
    damping_factor = visibilities.shape[2] * groups * total_channels / station_count
    coher_all = lax.all_to_all(coherencies, "dir", 2, 0, tiled=True)
    ends_p = jnp.take(start, stations[0], axis=2)
    ends_q = jnp.take(start, stations[1], axis=2)
    gain_p = jnp.transpose(ends_p, (1, 0, 2))[:, :, None, :]
    gain_q = jnp.transpose(ends_q, (1, 0, 2))[:, :, None, :]
    coher_f32 = jnp.transpose(coher_all, (1, 0, 2, 3)).astype(jnp.float32)
    first_model = jnp.sum(apply_gains(gain_p, coher_f32, gain_q), axis=1)
    first_residual = visibilities - first_model

    def direction_model(gain_now, coher_now):
        gain_p = jnp.take(gain_now, stations[0], axis=1)[:, None, :]
        gain_q = jnp.take(gain_now, stations[1], axis=1)[:, None, :]
        return apply_gains(gain_p, coher_now, gain_q)

    def sweep(step_index, state):
        gain_table, residual = state
        which = solve_order[step_index]
        coher_now = lax.dynamic_index_in_dim(coher_all, which, 0, keepdims=False).astype(
            jnp.float32
        )
        damp_value = damping[which].astype(jnp.float32) * damping_factor
        gain_start = gain_table[which]
        target = residual + direction_model(gain_start, coher_now)

        def iterate(round_index, gain_now):
            gain_p = jnp.take(gain_now, stations[0], axis=1)[:, None, :]
            gain_q = jnp.take(gain_now, stations[1], axis=1)[:, None, :]
            leading_endpoint, second = station_terms(gain_p, gain_q, coher_now, target)
            local_sums = (
                jax.ops.segment_sum(leading_endpoint.T, stations[0], station_count)
                + jax.ops.segment_sum(second.T, stations[1], station_count)
            ).T
            gathered_sums = lax.psum(local_sums, ("bl", "dir"))
            return solve_station(gathered_sums, gain_now, damp_value)

        rounds = jnp.clip(counts[which], 0, LM_ITERS)
        gain_final = lax.fori_loop(0, rounds, iterate, gain_start)
        residual = target - direction_model(gain_final, coher_now)
        return (gain_table.at[which].set(gain_final), residual)

    gain_table, residual = lax.fori_loop(0, SOLVED, sweep, (start, first_residual))
    own_width = station_count // groups
    gains = lax.dynamic_slice_in_dim(gain_table, lax.axis_index("bl") * own_width, own_width, 2)
    return (gains, residual)


def solution(mesh):
    return jax.shard_map(
        on_device,
        mesh=mesh,
        in_specs=(
            P(None, "dir", "bl"),
            P("dir", None, None, "bl"),
            P(None, None, "bl"),
            P(None, "bl"),
            P(),
            P(),
            P(),
        ),
        out_specs=(P(None, None, "bl"), P(None, "dir", "bl")),
        check_vma=False,
    )
```

profile of v0, /device:TPU:1, one launch (start us, length us, event | category | flops | bytes accessed | tf_op | source)
XLA Modules:
  0.0 847.1 jit_solution(9811879134477437065)
XLA Ops:
  0.6 1.6 copy.1122
  2.2 15.7 %all-to-all-start = ((bf16[2,8,16,256]{3,1,0,2:T(8,128)(2,1)}), bf16[2,8,16,256]{3,1,0,2:T(8,128)(2,1)S(1)}, u32[]{:S(2)}, u32[]{:S(2)}) async-start(bf16[2,8,16,256]{3,1,0,2:T(8,128)(2,1)} %copy.1122), calls=%async_computation | async-start | bytes 262144 | tf_op jit(solution)/shard_map/all_to_all | solution.py:81
  18.0 0.8 fusion.135
  18.8 0.9 copy.1120
  19.7 27.2 %all_gather.3 = f32[32,8,512]{0,1,2:T(8,128)S(1)} all-gather(f32[32,8,16]{0,1,2:T(8,128)S(1)} %copy.1120), channel_id=1, replica_groups=mesh['bl'=32,'dir'=16] {'bl'}, dimensions={2}, use_global_device_ids=true | all-gather | bytes 540672 | tf_op jit(solution)/shard_map/all_gather | solution.py:76
  47.1 0.9 copy.1133
  48.0 2.0 gather_fusion.7
  50.0 1.6 copy.1124
  51.6 2.0 gather_fusion.6
  53.6 1.6 copy.1121
  57.4 788.4 %while.42 = (s32[]{:T(128)}, f32[32,8,512]{2,1,0:T(8,128)S(1)}, f32[8,1,256]{2,1,0:T(1,128)S(1)}, s32[32]{0:T(128)S(1)}, s32[32]{0:T(128)S(1)}, /*index=5*/bf16[...) while((s32[]{:T(128)}, f32[32,8,512]{2,1,0:T(8,128)S(1)}, ...), condition=%wide.region_8.12_spmd, body=%wide.region_1.11_spmd.sunk | while | flops 253464 | bytes 1958014 | solution.py:121
  64.8 109.2 %while.43 = (s32[]{:T(128)}, f32[8,512]{1,0:T(8,128)S(1)}, s32[]{:T(128)}, s32[2,256]{1,0:T(2,128)S(1)}, f32[8,1,256]{2,1,0:T(1,128)S(1)}, /*index=5*/f32[8,1,25...) while((s32[]{:T(128)}, f32[8,512]{1,0:T(8,128)S(1)}, ...), condition=%wide.region_7.10_spmd, body=%wide.region_3.9_spmd.sunk | while | flops 160768 | bytes 1263793 | solution.py:117
  67.0 1.5 scatter_custom_fusion.11
  69.0 1.5 scatter_custom_fusion.10
  70.6 103.1 %psum.9 = f32[12,512]{1,0:T(8,128)S(1)} all-reduce(f32[12,512]{1,0:T(8,128)S(1)} %add_bitcast_fusion.2), channel_id=1, replica_groups=mesh['bl'=32,'dir'=16] {'bl','dir'}, use_global_device_ids=true, to_apply=%region_6.8 | all-reduce | flops 6144 | bytes 49152 | tf_op jit(solution)/shard_map/while/body/eval_jaxpr/while/body/psum | solution.py:113
  174.1 0.7 gather_fusion.4
  174.9 0.7 gather_fusion.5
  175.9 0.8 and_reduce_fusion.2
  184.6 212.3 %while.43 = (s32[]{:T(128)}, f32[8,512]{1,0:T(8,128)S(1)}, s32[]{:T(128)}, s32[2,256]{1,0:T(2,128)S(1)}, f32[8,1,256]{2,1,0:T(1,128)S(1)}, /*index=5*/f32[8,1,25...) while((s32[]{:T(128)}, f32[8,512]{1,0:T(8,128)S(1)}, ...), condition=%wide.region_7.10_spmd, body=%wide.region_3.9_spmd.sunk | while | flops 160768 | bytes 1263793 | solution.py:117
  186.8 1.5 scatter_custom_fusion.11
  188.8 1.5 scatter_custom_fusion.10
  190.4 100.7 %psum.9 = f32[12,512]{1,0:T(8,128)S(1)} all-reduce(f32[12,512]{1,0:T(8,128)S(1)} %add_bitcast_fusion.2), channel_id=1, replica_groups=mesh['bl'=32,'dir'=16] {'bl','dir'}, use_global_device_ids=true, to_apply=%region_6.8 | all-reduce | flops 6144 | bytes 49152 | tf_op jit(solution)/shard_map/while/body/eval_jaxpr/while/body/psum | solution.py:113
  293.6 1.5 scatter_custom_fusion.11
  295.5 1.5 scatter_custom_fusion.10
  297.2 99.4 %psum.9 = f32[12,512]{1,0:T(8,128)S(1)} all-reduce(f32[12,512]{1,0:T(8,128)S(1)} %add_bitcast_fusion.2), channel_id=1, replica_groups=mesh['bl'=32,'dir'=16] {'bl','dir'}, use_global_device_ids=true, to_apply=%region_6.8 | all-reduce | flops 6144 | bytes 49152 | tf_op jit(solution)/shard_map/while/body/eval_jaxpr/while/body/psum | solution.py:113
  397.0 0.7 gather_fusion.4
  397.8 0.7 gather_fusion.5
  398.8 0.8 and_reduce_fusion.2
  407.5 212.1 %while.43 = (s32[]{:T(128)}, f32[8,512]{1,0:T(8,128)S(1)}, s32[]{:T(128)}, s32[2,256]{1,0:T(2,128)S(1)}, f32[8,1,256]{2,1,0:T(1,128)S(1)}, /*index=5*/f32[8,1,25...) while((s32[]{:T(128)}, f32[8,512]{1,0:T(8,128)S(1)}, ...), condition=%wide.region_7.10_spmd, body=%wide.region_3.9_spmd.sunk | while | flops 160768 | bytes 1263793 | solution.py:117
  409.7 1.5 scatter_custom_fusion.11
  411.7 1.5 scatter_custom_fusion.10
  413.3 100.4 %psum.9 = f32[12,512]{1,0:T(8,128)S(1)} all-reduce(f32[12,512]{1,0:T(8,128)S(1)} %add_bitcast_fusion.2), channel_id=1, replica_groups=mesh['bl'=32,'dir'=16] {'bl','dir'}, use_global_device_ids=true, to_apply=%region_6.8 | all-reduce | flops 6144 | bytes 49152 | tf_op jit(solution)/shard_map/while/body/eval_jaxpr/while/body/psum | solution.py:113
  516.2 1.5 scatter_custom_fusion.11
  518.1 1.5 scatter_custom_fusion.10
  519.7 99.6 %psum.9 = f32[12,512]{1,0:T(8,128)S(1)} all-reduce(f32[12,512]{1,0:T(8,128)S(1)} %add_bitcast_fusion.2), channel_id=1, replica_groups=mesh['bl'=32,'dir'=16] {'bl','dir'}, use_global_device_ids=true, to_apply=%region_6.8 | all-reduce | flops 6144 | bytes 49152 | tf_op jit(solution)/shard_map/while/body/eval_jaxpr/while/body/psum | solution.py:113
  619.7 0.7 gather_fusion.4
  620.5 0.7 gather_fusion.5
  621.5 0.8 and_reduce_fusion.2
  630.2 212.2 %while.43 = (s32[]{:T(128)}, f32[8,512]{1,0:T(8,128)S(1)}, s32[]{:T(128)}, s32[2,256]{1,0:T(2,128)S(1)}, f32[8,1,256]{2,1,0:T(1,128)S(1)}, /*index=5*/f32[8,1,25...) while((s32[]{:T(128)}, f32[8,512]{1,0:T(8,128)S(1)}, ...), condition=%wide.region_7.10_spmd, body=%wide.region_3.9_spmd.sunk | while | flops 160768 | bytes 1263793 | solution.py:117
  632.5 1.5 scatter_custom_fusion.11
  634.4 1.5 scatter_custom_fusion.10
  636.0 100.5 %psum.9 = f32[12,512]{1,0:T(8,128)S(1)} all-reduce(f32[12,512]{1,0:T(8,128)S(1)} %add_bitcast_fusion.2), channel_id=1, replica_groups=mesh['bl'=32,'dir'=16] {'bl','dir'}, use_global_device_ids=true, to_apply=%region_6.8 | all-reduce | flops 6144 | bytes 49152 | tf_op jit(solution)/shard_map/while/body/eval_jaxpr/while/body/psum | solution.py:113
  739.0 1.5 scatter_custom_fusion.11
  740.9 1.5 scatter_custom_fusion.10
  742.5 99.6 %psum.9 = f32[12,512]{1,0:T(8,128)S(1)} all-reduce(f32[12,512]{1,0:T(8,128)S(1)} %add_bitcast_fusion.2), channel_id=1, replica_groups=mesh['bl'=32,'dir'=16] {'bl','dir'}, use_global_device_ids=true, to_apply=%region_6.8 | all-reduce | flops 6144 | bytes 49152 | tf_op jit(solution)/shard_map/while/body/eval_jaxpr/while/body/psum | solution.py:113
  842.5 0.7 gather_fusion.4
  843.3 0.7 gather_fusion.5
  844.3 0.8 and_reduce_fusion.2
  (579 shorter events, 43.3 us)
Async XLA Ops:
  0.6 46.2 %copy-start.4 = (f32[8]{0:T(128)S(1)}, f32[8]{0:T(128)}, u32[]{:S(2)}) copy-start(f32[8]{0:T(128)} %constant.188.clone.1) | copy-start | bytes 100
  2.2 53.1 %all-to-all-start = ((bf16[2,8,16,256]{3,1,0,2:T(8,128)(2,1)}), bf16[2,8,16,256]{3,1,0,2:T(8,128)(2,1)S(1)}, u32[]{:S(2)}, u32[]{:S(2)}) async-start(bf16[2,8,16,256]{3,1,0,2:T(8,128)(2,1)} %copy.1122), calls=%async_computation | async-start | bytes 262144 | tf_op jit(solution)/shard_map/all_to_all | solution.py:81
  55.2 2.1 copy-start.3
  55.2 2.1 copy-start
  55.3 2.1 copy-start.2
  55.3 2.1 copy-start.5
  55.3 2.1 copy-start.6
  55.3 2.1 copy-start.7
  845.8 1.3 copy-start.1
where the time goes:
time: 849 us; the launch traced here: 847 us
  blocking collectives  731 us (86%)
  local copies, waits for them, and re-layouts  49.5 us (6%)
  other arithmetic  35.1 us (4%)
  starting transfers between devices  15.7 us (2%)
  loops' own time  15.3 us (2%)
    psum x7, blocking collectives, iterate(): gathered_sums = lax.psum(local_sums, ('bl', 'dir'))  703 us
    all_gather x1, blocking collectives, on_device(): lax.all_gather(gain_offsets, 'bl', axis=2, tiled=True)  27.2 us
  transfers between devices with their start and end apart: 1, of which 0 were waited for; matrix products, arithmetic and copies ran while one was open for 1% of the time, Pallas kernels for 0%

commit v1 on v0

--- a/solution.py
+++ b/solution.py
@@ -110,7 +110,8 @@
                 jax.ops.segment_sum(leading_endpoint.T, stations[0], station_count)
                 + jax.ops.segment_sum(second.T, stations[1], station_count)
             ).T
-            gathered_sums = lax.psum(local_sums, ("bl", "dir"))
+            inner = lax.psum(local_sums, "dir")
+            gathered_sums = lax.psum(inner, "bl")
             return solve_station(gathered_sums, gain_now, damp_value)
 
         rounds = jnp.clip(counts[which], 0, LM_ITERS)

time: 849 us -> 1380 us (1.63)
  blocking collectives: 731 us -> 1260 us
    psum x7 -> x14, blocking collectives: 703 us -> 1240 us  [the longest x7 956 us: iterate(): gathered_sums = lax.psum(inner, 'bl')]
where the time goes in v1:
time: 1380 us
  blocking collectives  1260 us (91%)
  local copies, waits for them, and re-layouts  49.6 us (4%)
  other arithmetic  34.7 us (3%)
  starting transfers between devices  15.7 us (1%)
  loops' own time  15.3 us (1%)
    psum x7, blocking collectives, iterate(): gathered_sums = lax.psum(inner, 'bl')  956 us
    psum x7, blocking collectives, iterate(): inner = lax.psum(local_sums, 'dir')  280 us
  transfers between devices with their start and end apart: 1, of which 0 were waited for; matrix products, arithmetic and copies ran while one was open for 1% of the time, Pallas kernels for 0%

profile of v1, /device:TPU:1, one launch (start us, length us, event | category | flops | bytes accessed | tf_op | source)
XLA Modules:
  0.0 1379.8 jit_solution(3845699675552759697)
XLA Ops:
  0.6 1.6 copy.1122
  2.3 15.7 %all-to-all-start = ((bf16[2,8,16,256]{3,1,0,2:T(8,128)(2,1)}), bf16[2,8,16,256]{3,1,0,2:T(8,128)(2,1)S(1)}, u32[]{:S(2)}, u32[]{:S(2)}) async-start(bf16[2,8,16,256]{3,1,0,2:T(8,128)(2,1)} %copy.1122), calls=%async_computation | async-start | bytes 262144 | tf_op jit(solution)/shard_map/all_to_all | solution.py:81
  18.0 0.8 fusion.135
  18.8 0.9 copy.1120
  19.7 27.2 %all_gather.3 = f32[32,8,512]{0,1,2:T(8,128)S(1)} all-gather(f32[32,8,16]{0,1,2:T(8,128)S(1)} %copy.1120), channel_id=1, replica_groups=mesh['bl'=32,'dir'=16] {'bl'}, dimensions={2}, use_global_device_ids=true | all-gather | bytes 540672 | tf_op jit(solution)/shard_map/all_gather | solution.py:76
  47.1 0.9 copy.1133
  48.0 2.0 gather_fusion.7
  50.0 1.6 copy.1124
  51.6 2.0 gather_fusion.6
  53.6 1.6 copy.1121
  57.4 1321.1 %while.42 = (s32[]{:T(128)}, f32[32,8,512]{2,1,0:T(8,128)S(1)}, f32[8,1,256]{2,1,0:T(1,128)S(1)}, s32[32]{0:T(128)S(1)}, s32[32]{0:T(128)S(1)}, /*index=5*/bf16[...) while((s32[]{:T(128)}, f32[32,8,512]{2,1,0:T(8,128)S(1)}, ...), condition=%wide.region_9.13_spmd, body=%wide.region_1.12_spmd.sunk | while | flops 259608 | bytes 2007166 | solution.py:122
  64.8 180.6 %while.43 = (s32[]{:T(128)}, f32[8,512]{1,0:T(8,128)S(1)}, s32[]{:T(128)}, s32[2,256]{1,0:T(2,128)S(1)}, f32[8,1,256]{2,1,0:T(1,128)S(1)}, /*index=5*/f32[8,1,25...) while((s32[]{:T(128)}, f32[8,512]{1,0:T(8,128)S(1)}, ...), condition=%wide.region_8.11_spmd, body=%wide.region_3.10_spmd.sunk | while | flops 166912 | bytes 1312945 | solution.py:118
  67.0 1.5 scatter_custom_fusion.11
  69.0 1.5 scatter_custom_fusion.10
  70.6 43.2 %psum.18 = f32[12,512]{1,0:T(8,128)S(1)} all-reduce(f32[12,512]{1,0:T(8,128)S(1)} %add_bitcast_fusion.2), channel_id=1, replica_groups=mesh['bl'=32,'dir'=16] {'dir'}, use_global_device_ids=true, to_apply=%region_6.8 | all-reduce | flops 6144 | bytes 49152 | tf_op jit(solution)/shard_map/while/body/eval_jaxpr/while/body/psum | solution.py:113
  113.8 131.3 %psum.19 = f32[12,512]{1,0:T(8,128)S(1)} all-reduce(f32[12,512]{1,0:T(8,128)S(1)} %psum.18), channel_id=1, replica_groups=mesh['bl'=32,'dir'=16] {'bl'}, use_global_device_ids=true, to_apply=%region_7.9 | all-reduce | flops 6144 | bytes 49152 | tf_op jit(solution)/shard_map/while/body/eval_jaxpr/while/body/psum | solution.py:114
  246.3 0.7 gather_fusion.5
  247.4 0.7 and_reduce_fusion.2
  255.9 366.8 %while.43 = (s32[]{:T(128)}, f32[8,512]{1,0:T(8,128)S(1)}, s32[]{:T(128)}, s32[2,256]{1,0:T(2,128)S(1)}, f32[8,1,256]{2,1,0:T(1,128)S(1)}, /*index=5*/f32[8,1,25...) while((s32[]{:T(128)}, f32[8,512]{1,0:T(8,128)S(1)}, ...), condition=%wide.region_8.11_spmd, body=%wide.region_3.10_spmd.sunk | while | flops 166912 | bytes 1312945 | solution.py:118
  258.2 1.5 scatter_custom_fusion.11
  260.1 1.5 scatter_custom_fusion.10
  261.7 39.7 %psum.18 = f32[12,512]{1,0:T(8,128)S(1)} all-reduce(f32[12,512]{1,0:T(8,128)S(1)} %add_bitcast_fusion.2), channel_id=1, replica_groups=mesh['bl'=32,'dir'=16] {'dir'}, use_global_device_ids=true, to_apply=%region_6.8 | all-reduce | flops 6144 | bytes 49152 | tf_op jit(solution)/shard_map/while/body/eval_jaxpr/while/body/psum | solution.py:113
  301.4 137.7 %psum.19 = f32[12,512]{1,0:T(8,128)S(1)} all-reduce(f32[12,512]{1,0:T(8,128)S(1)} %psum.18), channel_id=1, replica_groups=mesh['bl'=32,'dir'=16] {'bl'}, use_global_device_ids=true, to_apply=%region_7.9 | all-reduce | flops 6144 | bytes 49152 | tf_op jit(solution)/shard_map/while/body/eval_jaxpr/while/body/psum | solution.py:114
  441.6 1.5 scatter_custom_fusion.11
  443.5 1.5 scatter_custom_fusion.10
  445.2 39.6 %psum.18 = f32[12,512]{1,0:T(8,128)S(1)} all-reduce(f32[12,512]{1,0:T(8,128)S(1)} %add_bitcast_fusion.2), channel_id=1, replica_groups=mesh['bl'=32,'dir'=16] {'dir'}, use_global_device_ids=true, to_apply=%region_6.8 | all-reduce | flops 6144 | bytes 49152 | tf_op jit(solution)/shard_map/while/body/eval_jaxpr/while/body/psum | solution.py:113
  484.8 137.7 %psum.19 = f32[12,512]{1,0:T(8,128)S(1)} all-reduce(f32[12,512]{1,0:T(8,128)S(1)} %psum.18), channel_id=1, replica_groups=mesh['bl'=32,'dir'=16] {'bl'}, use_global_device_ids=true, to_apply=%region_7.9 | all-reduce | flops 6144 | bytes 49152 | tf_op jit(solution)/shard_map/while/body/eval_jaxpr/while/body/psum | solution.py:114
  624.7 0.7 and_reduce_fusion.2
  633.3 365.7 %while.43 = (s32[]{:T(128)}, f32[8,512]{1,0:T(8,128)S(1)}, s32[]{:T(128)}, s32[2,256]{1,0:T(2,128)S(1)}, f32[8,1,256]{2,1,0:T(1,128)S(1)}, /*index=5*/f32[8,1,25...) while((s32[]{:T(128)}, f32[8,512]{1,0:T(8,128)S(1)}, ...), condition=%wide.region_8.11_spmd, body=%wide.region_3.10_spmd.sunk | while | flops 166912 | bytes 1312945 | solution.py:118
  635.5 1.5 scatter_custom_fusion.11
  637.5 1.5 scatter_custom_fusion.10
  639.1 39.1 %psum.18 = f32[12,512]{1,0:T(8,128)S(1)} all-reduce(f32[12,512]{1,0:T(8,128)S(1)} %add_bitcast_fusion.2), channel_id=1, replica_groups=mesh['bl'=32,'dir'=16] {'dir'}, use_global_device_ids=true, to_apply=%region_6.8 | all-reduce | flops 6144 | bytes 49152 | tf_op jit(solution)/shard_map/while/body/eval_jaxpr/while/body/psum | solution.py:113
  678.2 137.4 %psum.19 = f32[12,512]{1,0:T(8,128)S(1)} all-reduce(f32[12,512]{1,0:T(8,128)S(1)} %psum.18), channel_id=1, replica_groups=mesh['bl'=32,'dir'=16] {'bl'}, use_global_device_ids=true, to_apply=%region_7.9 | all-reduce | flops 6144 | bytes 49152 | tf_op jit(solution)/shard_map/while/body/eval_jaxpr/while/body/psum | solution.py:114
  818.1 1.5 scatter_custom_fusion.11
  820.0 1.5 scatter_custom_fusion.10
  821.7 39.9 %psum.18 = f32[12,512]{1,0:T(8,128)S(1)} all-reduce(f32[12,512]{1,0:T(8,128)S(1)} %add_bitcast_fusion.2), channel_id=1, replica_groups=mesh['bl'=32,'dir'=16] {'dir'}, use_global_device_ids=true, to_apply=%region_6.8 | all-reduce | flops 6144 | bytes 49152 | tf_op jit(solution)/shard_map/while/body/eval_jaxpr/while/body/psum | solution.py:113
  861.6 137.1 %psum.19 = f32[12,512]{1,0:T(8,128)S(1)} all-reduce(f32[12,512]{1,0:T(8,128)S(1)} %psum.18), channel_id=1, replica_groups=mesh['bl'=32,'dir'=16] {'bl'}, use_global_device_ids=true, to_apply=%region_7.9 | all-reduce | flops 6144 | bytes 49152 | tf_op jit(solution)/shard_map/while/body/eval_jaxpr/while/body/psum | solution.py:114
  1000.9 0.7 and_reduce_fusion.2
  1009.5 365.6 %while.43 = (s32[]{:T(128)}, f32[8,512]{1,0:T(8,128)S(1)}, s32[]{:T(128)}, s32[2,256]{1,0:T(2,128)S(1)}, f32[8,1,256]{2,1,0:T(1,128)S(1)}, /*index=5*/f32[8,1,25...) while((s32[]{:T(128)}, f32[8,512]{1,0:T(8,128)S(1)}, ...), condition=%wide.region_8.11_spmd, body=%wide.region_3.10_spmd.sunk | while | flops 166912 | bytes 1312945 | solution.py:118
  1011.8 1.5 scatter_custom_fusion.11
  1013.7 1.5 scatter_custom_fusion.10
  1015.3 39.1 %psum.18 = f32[12,512]{1,0:T(8,128)S(1)} all-reduce(f32[12,512]{1,0:T(8,128)S(1)} %add_bitcast_fusion.2), channel_id=1, replica_groups=mesh['bl'=32,'dir'=16] {'dir'}, use_global_device_ids=true, to_apply=%region_6.8 | all-reduce | flops 6144 | bytes 49152 | tf_op jit(solution)/shard_map/while/body/eval_jaxpr/while/body/psum | solution.py:113
  1054.4 137.4 %psum.19 = f32[12,512]{1,0:T(8,128)S(1)} all-reduce(f32[12,512]{1,0:T(8,128)S(1)} %psum.18), channel_id=1, replica_groups=mesh['bl'=32,'dir'=16] {'bl'}, use_global_device_ids=true, to_apply=%region_7.9 | all-reduce | flops 6144 | bytes 49152 | tf_op jit(solution)/shard_map/while/body/eval_jaxpr/while/body/psum | solution.py:114
  1194.3 1.5 scatter_custom_fusion.11
  1196.3 1.5 scatter_custom_fusion.10
  1197.9 39.6 %psum.18 = f32[12,512]{1,0:T(8,128)S(1)} all-reduce(f32[12,512]{1,0:T(8,128)S(1)} %add_bitcast_fusion.2), channel_id=1, replica_groups=mesh['bl'=32,'dir'=16] {'dir'}, use_global_device_ids=true, to_apply=%region_6.8 | all-reduce | flops 6144 | bytes 49152 | tf_op jit(solution)/shard_map/while/body/eval_jaxpr/while/body/psum | solution.py:113
  1237.5 137.4 %psum.19 = f32[12,512]{1,0:T(8,128)S(1)} all-reduce(f32[12,512]{1,0:T(8,128)S(1)} %psum.18), channel_id=1, replica_groups=mesh['bl'=32,'dir'=16] {'bl'}, use_global_device_ids=true, to_apply=%region_7.9 | all-reduce | flops 6144 | bytes 49152 | tf_op jit(solution)/shard_map/while/body/eval_jaxpr/while/body/psum | solution.py:114
  1377.1 0.7 and_reduce_fusion.2
  (586 shorter events, 48.3 us)
Async XLA Ops:
  0.6 46.2 %copy-start.4 = (f32[8]{0:T(128)S(1)}, f32[8]{0:T(128)}, u32[]{:S(2)}) copy-start(f32[8]{0:T(128)} %constant.188.clone.1) | copy-start | bytes 100
  2.3 53.1 %all-to-all-start = ((bf16[2,8,16,256]{3,1,0,2:T(8,128)(2,1)}), bf16[2,8,16,256]{3,1,0,2:T(8,128)(2,1)S(1)}, u32[]{:S(2)}, u32[]{:S(2)}) async-start(bf16[2,8,16,256]{3,1,0,2:T(8,128)(2,1)} %copy.1122), calls=%async_computation | async-start | bytes 262144 | tf_op jit(solution)/shard_map/all_to_all | solution.py:81
  55.2 2.1 copy-start.3
  55.2 2.1 copy-start
  55.3 2.1 copy-start.2
  55.3 2.1 copy-start.5
  55.3 2.1 copy-start.6
  55.3 2.1 copy-start.7
  1378.5 1.3 copy-start.1
